TPU v7x, 256 devices: a whole 4x4x8 slice. The times are simulated.
256 devices in a mesh: seq: 64 (over x, z, core), head: 4 (over y).
Axes of the slice: x: 4, y: 4, z: 8, core: 2. Of those that a mesh axis runs over, the one named last changes fastest.
Arguments:
- latent: bfloat16 [64, 16, 1024], P('seq'), may hold values from -6 to 6
- stem_weight: bfloat16 [192, 3072], replicated, may hold values from -0.4375 to 0.4375
- stem_bias: float32 [3072], replicated, may hold values from -6 to 6
- mod_shift: float32 [3072], replicated, may hold values from -3 to 3
- mod_scale: float32 [3072], replicated, may hold values from -3 to 3
- qkv_weight: bfloat16 [3072, 3, 12, 128], P(None, None, 'head'), may hold values from -0.109375 to 0.109375
- q_gain: float32 [128], replicated, may hold values from 0.1 to 1.9
- k_gain: float32 [128], replicated, may hold values from 0.1 to 1.9
- tile_lists: int32 [128, 4], replicated, may hold values from 0 to 127, as said below
- out_grad: bfloat16 [16384, 12, 128], P('seq', 'head'), may hold values from -0.125 to 0.125
Outputs:
- qkv_weight_grad: float32 [3072, 3, 12, 128], P('seq', None, 'head')
- stem_weight_grad: float32 [192, 3072], P(None, 'head')
- vector_grad: float32 [3, 3072], P(None, 'head')
Inputs may be any that keep to these rules, and one draw needn't show every extreme that they name: `tile_lists`: row b holds 4 different tiles of tile b's own group of 8 tiles (b - b % 8 to b - b % 8 + 7), the first being b itself.
All inputs are finite; a program needn't handle non-finite values.
Results may differ from a plain program's by a relative error of at most 0.0078.
Values may be sent and summed in bfloat16 or wider, within the bound.
No kernel may reach another device: no remote copies, remote signals or barrier semaphores. Data moves between devices by JAX's collectives and lax.ppermute only.
A program may use at most 128 MiB of HBM per device.

v0:
```python
import jax
import jax.numpy as jnp
from jax import lax
from jax.sharding import PartitionSpec as P

TT = 2
TS = 8
KNB = 4
HG = 32
WG = 16
ln_eps = 1e-06


def swapped(value, axis, distance):
    mask = 2**distance
    pairs = [(source, source ^ mask) for source in range(lax.axis_size(axis))]
    return lax.ppermute(value, axis, pairs)


def from_behind(value, axis, steps):
    count = lax.axis_size(axis)
    first, last = (max(0, -steps), min(count, count - steps))
    return lax.ppermute(value, axis, [(source, source + steps) for source in range(first, last)])


def frames_to_tiles(blocks, row_total, col_total, tile_side):
    frames = blocks.shape[0]
    remain = blocks.shape[2:]
    shaped = blocks.reshape(
        (frames, row_total // tile_side, tile_side, col_total // tile_side, tile_side) + remain
    )
    shaped = jnp.transpose(shaped, (1, 3, 0, 2, 4) + tuple(range(5, 5 + len(remain))))
    return shaped.reshape(
        (row_total // tile_side * (col_total // tile_side), frames * tile_side * tile_side) + remain
    )


def tiles_to_frames(blocks, frames, row_total, col_total, tile_side):
    remain = blocks.shape[2:]
    shaped = blocks.reshape(
        (row_total // tile_side, col_total // tile_side, frames, tile_side, tile_side) + remain
    )
    shaped = jnp.transpose(shaped, (2, 0, 3, 1, 4) + tuple(range(5, 5 + len(remain))))
    return shaped.reshape((frames, row_total * col_total) + remain)


def qk_norm(raw_values, gain_vector):
    return (
        raw_values
        * lax.rsqrt(jnp.mean(raw_values * raw_values, -1, keepdims=True) + ln_eps)
        * gain_vector
    )


def norm_back(feature_grad, normed, inv_std, mod_scale):
    scaled = feature_grad * (1.0 + mod_scale)
    return (
        scaled
        - jnp.mean(scaled, -1, keepdims=True)
        - normed * jnp.mean(scaled * normed, -1, keepdims=True)
    ) * inv_std


def attend(queries, out_grads, key_vals, values, score_scale):
    scores = (
        jnp.einsum("brhe,bmhe->bhrm", queries, key_vals, preferred_element_type=jnp.float32)
        * score_scale
    )
    weights = jnp.exp(scores)
    probability = weights / jnp.sum(weights, axis=-1, keepdims=True)
    rounded = probability.astype(jnp.bfloat16)
    slopes = jnp.einsum("brhe,bmhe->bhrm", out_grads, values, preferred_element_type=jnp.float32)
    centre = jnp.sum(probability * slopes, axis=-1, keepdims=True)
    shaped = (probability * (slopes - centre)).astype(jnp.bfloat16)
    query_grad = (
        jnp.einsum("bhrm,bmhe->brhe", shaped, key_vals, preferred_element_type=jnp.float32)
        * score_scale
    )
    key_grad = (
        jnp.einsum("bhrm,brhe->bmhe", shaped, queries, preferred_element_type=jnp.float32)
        * score_scale
    )
    value_grad = jnp.einsum(
        "bhrm,brhe->bmhe", rounded, out_grads, preferred_element_type=jnp.float32
    )
    return (query_grad, key_grad, value_grad)


def group_share(blocks):
    seq_place = lax.axis_index("seq")
    for bit_index in range((2 * TT).bit_length() - 1):
        partner = swapped(blocks, "seq", bit_index)
        is_lower = seq_place // (1 << bit_index) % 2 == 0
        first_half = jnp.where(is_lower, blocks, partner)
        second_half = jnp.where(is_lower, partner, blocks)
        blocks = jnp.concatenate([first_half, second_half], 0)
    return blocks


def group_return(blocks):
    seq_place = lax.axis_index("seq")
    for bit_index in reversed(range((2 * TT).bit_length() - 1)):
        half_size = blocks.shape[0] // 2
        is_lower = seq_place // (1 << bit_index) % 2 == 0
        kept_part = jnp.where(is_lower, blocks[:half_size], blocks[half_size:])
        sent_part = jnp.where(is_lower, blocks[half_size:], blocks[:half_size])
        blocks = kept_part + swapped(sent_part, "seq", bit_index)
    return blocks[0]


def seq_total(stem_part, vector_part):
    return lax.psum((stem_part, vector_part), "seq")


def per_device(
    latent,
    stem_weight,
    stem_bias,
    mod_shift,
    mod_scale,
    qkv_weight,
    q_gain,
    k_gain,
    tile_lists,
    out_grad,
):
    half_rows = HG // 2
    tok_count = half_rows * WG
    frame_tokens = HG * WG
    model_width = qkv_weight.shape[0]
    heads_here = qkv_weight.shape[2]
    head_dim = qkv_weight.shape[3]
    score_scale = head_dim ** (-0.5)
    before = from_behind(latent, "seq", 2)
    after = from_behind(latent, "seq", -2)
    padded = jnp.concatenate([before, latent, after], 0)
    channels = latent.shape[1]
    patches = padded.reshape(3, channels, half_rows, 2, WG, 2)
    patches = jnp.transpose(patches, (2, 4, 0, 1, 3, 5)).reshape(tok_count, 12 * channels)
    embedded = jnp.dot(patches, stem_weight, preferred_element_type=jnp.float32) + stem_bias
    centred = embedded - jnp.mean(embedded, -1, keepdims=True)
    inv_std = lax.rsqrt(jnp.mean(centred * centred, -1, keepdims=True) + ln_eps)
    normed = centred * inv_std
    hidden = (normed * (1.0 + mod_scale) + mod_shift).astype(jnp.bfloat16)
    columns = 3 * heads_here * head_dim
    flat_weight = qkv_weight.reshape(model_width, columns)
    projected = jnp.dot(hidden, flat_weight, preferred_element_type=jnp.float32).reshape(
        tok_count, 3, heads_here, head_dim
    )
    q_normed, q_back = jax.vjp(lambda raw_values: qk_norm(raw_values, q_gain), projected[:, 0])
    k_normed, k_back = jax.vjp(lambda raw_values: qk_norm(raw_values, k_gain), projected[:, 1])
    queries = q_normed.astype(jnp.bfloat16)
    key_vals = k_normed.astype(jnp.bfloat16)
    values = projected[:, 2].astype(jnp.bfloat16)
    seq_place = lax.axis_index("seq")
    group_devs = 2 * TT
    my_group = seq_place // group_devs
    my_half = seq_place % 2
    tiles_group = HG // TS * (WG // TS)
    half_tiles = tiles_group // 2
    local_lists = (
        lax.dynamic_slice_in_dim(tile_lists, my_group * tiles_group, tiles_group, 0)
        - my_group * tiles_group
    )
    shared = group_share(jnp.stack([key_vals, values], 1)[None])
    shared = shared.reshape((TT, frame_tokens) + shared.shape[2:])
    tiles = frames_to_tiles(shared, HG, WG, TS)
    tile_len = tiles.shape[1]
    my_lists = lax.dynamic_slice_in_dim(local_lists, my_half * half_tiles, half_tiles, 0)
    near_tiles = jnp.take(tiles, my_lists.reshape(-1), axis=0)
    near_tiles = near_tiles.reshape(half_tiles, KNB * tile_len, 2, heads_here, head_dim)
    own_queries = frames_to_tiles(queries[None], half_rows, WG, TS)
    own_grads = frames_to_tiles(out_grad[None], half_rows, WG, TS)
    query_part, key_part, value_part = attend(
        own_queries, own_grads, near_tiles[:, :, 0], near_tiles[:, :, 1], score_scale
    )
    query_grad = tiles_to_frames(query_part, 1, half_rows, WG, TS)[0]
    pair_part = jnp.stack([key_part, value_part], 2).reshape(
        half_tiles * KNB, tile_len, 2, heads_here, head_dim
    )
    pair_tiles = (
        jnp.zeros((tiles_group, tile_len, 2, heads_here, head_dim), jnp.float32)
        .at[my_lists.reshape(-1)]
        .add(pair_part)
    )
    framed = tiles_to_frames(pair_tiles, TT, HG, WG, TS)
    returned = group_return(framed.reshape((group_devs, tok_count) + framed.shape[2:]))
    key_grad = returned[:, 0]
    value_grad = returned[:, 1]
    raw_q = q_back(query_grad)[0]
    raw_k = k_back(key_grad)[0]
    mixed_grad = (
        jnp.stack([raw_q, raw_k, value_grad], 1).astype(jnp.bfloat16).reshape(tok_count, columns)
    )
    weight_grad = lax.psum_scatter(
        lax.dot_general(
            hidden, mixed_grad, (((0,), (0,)), ((), ())), preferred_element_type=jnp.float32
        ),
        "seq",
        scatter_dimension=0,
        tiled=True,
    )
    weight_grad = weight_grad.reshape(-1, 3, heads_here, head_dim)
    feature_grad = lax.dot_general(
        mixed_grad, flat_weight, (((1,), (1,)), ((), ())), preferred_element_type=jnp.float32
    )
    patch_rows = patches.astype(jnp.float32)
    feature_grad = lax.psum(feature_grad, "head")
    embed_grad = norm_back(feature_grad, normed, inv_std, mod_scale)
    share_cols = model_width // lax.axis_size("head")
    offset = lax.axis_index("head") * share_cols
    grad_slice = lax.dynamic_slice_in_dim(feature_grad, offset, share_cols, 1)
    normed_slice = lax.dynamic_slice_in_dim(normed, offset, share_cols, 1)
    embed_slice = lax.dynamic_slice_in_dim(embed_grad, offset, share_cols, 1)
    stem_part = lax.dot_general(
        patch_rows, embed_slice, (((0,), (0,)), ((), ())), precision=lax.Precision.HIGHEST
    )
    vector_part = jnp.stack(
        [jnp.sum(grad_slice, 0), jnp.sum(grad_slice * normed_slice, 0), jnp.sum(embed_slice, 0)]
    )
    stem_grad, vector_grad = seq_total(stem_part, vector_part)
    return (weight_grad, stem_grad, vector_grad)


def solution(mesh):
    return jax.shard_map(
        per_device,
        mesh=mesh,
        in_specs=(
            P("seq", None, None),
            P(),
            P(),
            P(),
            P(),
            P(None, None, "head", None),
            P(),
            P(),
            P(),
            P("seq", "head", None),
        ),
        out_specs=(P("seq", None, "head", None), P(None, "head"), P(None, "head")),
        check_vma=False,
    )
```

profile of v0, /device:TPU:8, one launch (start us, length us, event | category | flops | bytes accessed | tf_op | source)
XLA Modules:
  0.0 514.7 jit_solution(13901229938263370222)
XLA Ops:
  8.1 4.0 collective-permute-start
  14.0 10.3 %copy.44 = bf16[3072,3,3,128]{0,3,2,1:T(8,128)(2,1)} copy(bf16[3072,3,3,128]{3,0,2,1:T(8,128)(2,1)} %param.15) | data formatting | bytes 14155776 | tf_op args[5]
  31.3 2.3 fusion
  36.9 2.9 collective-permute-start.3
  40.2 17.6 %collective-permute-done.3 = bf16[2,256,2,3,128]{4,1,3,2,0:T(8,128)(2,1)} collective-permute-done((bf16[2,256,2,3,128]{4,1,3,2,0:T(8,128)(2,1)S(1)}, bf16[2,256,2,3,128]{4,1,3,2,0:T(8,128)(2,1)}, u32[]{:S(2)}, u32[]{:S(2)}) %collective-permute-start.3) | collective-permute-done | bytes 786464 | tf_op jit(solution)/shard_map/ppermute | solution.py:17
  59.7 2.6 gather_fusion
  62.3 2.3 copy.48
  67.5 3.3 convolution_bitcast_fusion.1
  70.8 2.1 fusion.4
  73.0 1.9 copy.54
  76.7 2.3 copy.53
  79.0 3.3 pad_maximum_fusion
  82.3 3.1 copy.55
  85.7 9.3 %scatter_fusion = f32[8,128,2,3,128]{4,1,3,2,0:T(8,128)S(1)} fusion(f32[8,128,2,3,128]{4,1,3,2,0:T(8,128)S(1)} %broadcast_in_dim.47, s32[16]{0:T(128)S(1)} %fusion.24, f32[16,128,2,3,128]{4,1,3,2,0:T(8,128)} %copy.55), kind=kCustom, calls=%fused_computation.1 | custom fusion | flops 1572864 | bytes 18874432 | tf_op jit(solution)/shard_map/scatter-add | solution.py:184
  97.7 34.2 %collective-permute-done.4 = f32[2,256,2,3,128]{4,1,3,2,0:T(8,128)S(1)} collective-permute-done((f32[2,256,2,3,128]{4,1,3,2,0:T(8,128)S(1)}, f32[2,256,2,3,128]{4,1,3,2,0:T(8,128)S(1)}, u32[]{:S(2)}, u32[]{:S(2)}) %collective-permute-start.4) | collective-permute-done | bytes 1572896 | tf_op jit(solution)/shard_map/ppermute | solution.py:17
  136.3 4.0 convolution_bitcast_fusion
  140.6 2.1 maximum_convert_fusion
  142.7 2.1 copy.59
  144.8 8.4 %fusion.14 = f32[3072,1152]{1,0:T(8,128)} fusion(bf16[256,1152]{0,1:T(8,128)(2,1)} %bitcast.148, f32[256,3072]{1,0:T(8,128)S(1)} %copy-done.5, f32[3072]{0:T(1024)S(1)} %copy-done.17, f32[3072]{0:T(1024)S(1)} %broadcast_add_fusion), kind=kOutput, calls=%fused_computation.48 | convolution fusion | flops 1814298624 | bytes 17915904 | tf_op jit(solution)/shard_map/dot_general | solution.py:196
  153.3 70.6 %all-reduce.3.cloned.1.call-done = f32[256,3072]{1,0:T(8,128)} async-done(((f32[256,3072]{1,0:T(8,128)}), f32[256,3072]{1,0:T(8,128)}) %all-reduce.3.cloned.1.call-update) | async-done | bytes 3145744 | tf_op jit(solution)/shard_map/psum | solution.py:208
  223.9 2.9 fusion.26
  229.9 252.3 %psum.23 = f32[3,768]{1,0:T(4,128)} all-reduce(f32[3,768]{1,0:T(4,128)S(1)} %pad_maximum_fusion.4), channel_id=1, replica_groups=mesh['seq'=64,'head'=4] {'seq'}, use_global_device_ids=true, to_apply=%region_17.18 | all-reduce | flops 2304 | bytes 18432 | tf_op jit(solution)/shard_map/psum | solution.py:112
  484.0 21.3 %all-reduce.5.cloned.1.call-done = f32[192,768]{1,0:T(8,128)} async-done(((f32[192,768]{1,0:T(8,128)}), f32[192,768]{1,0:T(8,128)}) %all-reduce.5.cloned.1.call-update) | async-done | bytes 589840 | tf_op jit(solution)/shard_map/psum | solution.py:112
  505.3 1.9 copy.73
  (133 shorter events, 31.6 us)
Async XLA Ops:
  8.0 19.1 %copy-start = (bf16[192,3072]{1,0:T(8,128)(2,1)S(1)}, bf16[192,3072]{1,0:T(8,128)(2,1)}, u32[]{:S(2)}) copy-start(bf16[192,3072]{1,0:T(8,128)(2,1)} %param.11) | copy-start | bytes 3538948
  8.0 215.9 %all-reduce.3.cloned.1.call-start = ((), (), s32[]{:S(2)}) async-start(), calls=%async_computation.2 | async-start | bytes 6291456 | tf_op jit(solution)/shard_map/psum | solution.py:208
  8.1 16.3 %collective-permute-start = (bf16[1,16,1024]{2,1,0:T(8,128)(2,1)}, bf16[1,16,1024]{2,1,0:T(8,128)(2,1)S(1)}, u32[]{:S(2)}, u32[]{:S(2)}) collective-permute-start(bf16[1,16,1024]{2,1,0:T(8,128)(2,1)} %param.10), channel_id=1, source_target_pairs={{0,8},{4,12},{8,16},{12,20},{16,24},{20,28},{24,32},{28,36},{32,40... | collective-permute-start | bytes 98312 | tf_op jit(solution)/shard_map/ppermute | solution.py:23
  12.0 12.3 %collective-permute-start.1 = (bf16[1,16,1024]{2,1,0:T(8,128)(2,1)}, bf16[1,16,1024]{2,1,0:T(8,128)(2,1)S(1)}, u32[]{:S(2)}, u32[]{:S(2)}) collective-permute-start(bf16[1,16,1024]{2,1,0:T(8,128)(2,1)} %param.10), channel_id=1, source_target_pairs={{8,0},{12,4},{16,8},{20,12},{24,16},{28,20},{32,24},{36,28},{40,32... | collective-permute-start | bytes 98312 | tf_op jit(solution)/shard_map/ppermute | solution.py:23
  14.0 10.3 %copy-start.18 = (bf16[1,16,1024]{2,1,0:T(8,128)(2,1)S(1)}, bf16[1,16,1024]{2,1,0:T(8,128)(2,1)}, u32[]{:S(2)}) copy-start(bf16[1,16,1024]{2,1,0:T(8,128)(2,1)} %param.10) | copy-start | bytes 98308
  24.3 2.8 copy-start.19
  27.1 3.3 slice-start.2
  27.8 3.5 slice-start.3
  31.3 3.4 copy-start.20
  33.9 6.0 %copy-start.21 = (f32[128]{0:T(128)S(1)}, f32[128]{0:T(128)}, u32[]{:S(2)}) copy-start(f32[128]{0:T(128)} %param.16) | copy-start | bytes 1540
  34.9 1.8 collective-permute-start.2
  35.6 29.5 %copy-start.15 = (bf16[2,2,1,8,8,3,128]{6,4,3,5,1,0,2:T(8,128)(2,1)}, bf16[2,2,1,8,8,3,128]{6,4,3,5,1,0,2:T(8,128)(2,1)S(1)}, u32[]{:S(2)}) copy-start(bf16[2,2,1,8,8,3,128]{6,4,3,5,1,0,2:T(8,128)(2,1)S(1)} %copy.51) | copy-start | bytes 589828
  36.9 20.9 %collective-permute-start.3 = (bf16[2,256,2,3,128]{4,1,3,2,0:T(8,128)(2,1)S(1)}, bf16[2,256,2,3,128]{4,1,3,2,0:T(8,128)(2,1)}, u32[]{:S(2)}, u32[]{:S(2)}) collective-permute-start(bf16[2,256,2,3,128]{4,1,3,2,0:T(8,128)(2,1)S(1)} %pad_maximum_fusion.2), channel_id=1, source_target_pairs={{0,8},{4,12},{8,0},{12,4},{16,24},{20,28},{24,16},{28,20},{32,40},... | collective-permute-start | bytes 2359304 | tf_op jit(solution)/shard_map/ppermute | solution.py:17
  95.7 36.6 %copy-start.12 = (bf16[4,3,64,512]{3,2,1,0:T(8,128)(2,1)S(1)}, bf16[4,3,64,512]{3,2,1,0:T(8,128)(2,1)}, u32[]{:S(2)}) copy-start(bf16[4,3,64,512]{3,2,1,0:T(8,128)(2,1)} %copy-done.11) | copy-start | bytes 2359300
  95.9 36.0 %collective-permute-start.4 = (f32[2,256,2,3,128]{4,1,3,2,0:T(8,128)S(1)}, f32[2,256,2,3,128]{4,1,3,2,0:T(8,128)S(1)}, u32[]{:S(2)}, u32[]{:S(2)}) collective-permute-start(f32[2,256,2,3,128]{4,1,3,2,0:T(8,128)S(1)} %copy.57), channel_id=1, source_target_pairs={{0,8},{4,12},{8,0},{12,4},{16,24},{20,28},{24,16},{28,20},{32,40},... | collective-permute-start | bytes 4718600 | tf_op jit(solution)/shard_map/ppermute | solution.py:17
  131.9 4.5 slice-start
  132.2 2.6 copy-start.9
  132.2 4.1 slice-start.1
  132.2 2.4 collective-permute-start.5
  140.3 4.5 copy-start.5
  140.3 341.9 %reduce-scatter.2.cloned.1.call-start = ((), (), s32[]{:S(2)}) async-start(), calls=%async_computation.1 | async-start | bytes 14376960 | tf_op jit(solution)/shard_map/reduce_scatter | solution.py:195
  153.2 70.7 %copy-start.3 = (f32[256,3072]{1,0:T(8,128)S(1)}, f32[256,3072]{1,0:T(8,128)}, u32[]{:S(2)}) copy-start(f32[256,3072]{1,0:T(8,128)} %copy-done.2) | copy-start | bytes 9437188
  153.2 352.1 %all-reduce.5.cloned.1.call-start = ((), (), s32[]{:S(2)}) async-start(), calls=%async_computation.3 | async-start | bytes 1179648 | tf_op jit(solution)/shard_map/psum | solution.py:112
  226.8 280.5 %copy-start.1 = (bf16[192,3072]{1,0:T(8,128)(2,1)S(1)}, bf16[192,3072]{1,0:T(8,128)(2,1)}, u32[]{:S(2)}) copy-start(bf16[192,3072]{1,0:T(8,128)(2,1)} %param.11) | copy-start | bytes 3538948
  (12 other events, 18.6 us)
Sparse Core Ops, SparseCore 0:
  140.5 83.3 all-reduce.2
Sparse Core Ops, SparseCore 1:
  153.3 168.1 reduce-scatter.1
  325.3 179.9 all-reduce.4
where the time goes:
time: 516 us; the launch traced here: 515 us
  blocking collectives  252 us (49%)
  waiting for transfers between devices  145 us (28%)
  local copies, waits for them, and re-layouts  40.5 us (8%)
  other arithmetic  28 us (5%)
  matrix products  22.3 us (4%)
  between operations  16.1 us (3%)
  starting transfers between devices  10.5 us (2%)
    psum x1, blocking collectives, seq_total(): return lax.psum((stem_part, vector_part), 'seq')  252 us
    psum x1, waiting for transfers between devices, per_device(): feature_grad = lax.psum(feature_grad, 'head')  70.6 us
    ppermute x4, waiting for transfers between devices, swapped(): return lax.ppermute(value, axis, pairs)  52.9 us
    psum x1, waiting for transfers between devices, seq_total(): return lax.psum((stem_part, vector_part), 'seq')  21.3 us
    unnamed x59, local copies, waits for them, and re-layouts  20.7 us
  transfers between devices with their start and end apart: 9, of which 5 were waited for; matrix products, arithmetic and copies ran while one was open for 6% of the time, Pallas kernels for 0%

commit v1 on v0

--- a/solution.py
+++ b/solution.py
@@ -205,7 +205,7 @@
         mixed_grad, flat_weight, (((1,), (1,)), ((), ())), preferred_element_type=jnp.float32
     )
     patch_rows = patches.astype(jnp.float32)
-    feature_grad = lax.psum(feature_grad, "head")
+    feature_grad = jnp.sum(lax.all_gather(feature_grad, "head"), axis=0)
     embed_grad = norm_back(feature_grad, normed, inv_std, mod_scale)
     share_cols = model_width // lax.axis_size("head")
     offset = lax.axis_index("head") * share_cols

time: 516 us -> 542 us (1.050)
  waiting for transfers between devices: 145 us -> 165 us
  other arithmetic: 28 us -> 35.9 us
    all_gather x0 -> x1, waiting for transfers between devices: none -> 112 us  [per_device(): feature_grad = jnp.sum(lax.all_gather(feature_grad, 'head'), axis=0)]
    psum x1 -> x0, waiting for transfers between devices: 70.6 us -> none  [per_device(): feature_grad = lax.psum(feature_grad, 'head')]
    psum x1, waiting for transfers between devices: 21.3 us -> 0.01 us  [seq_total(): return lax.psum((stem_part, vector_part), 'seq')]
    reduce_sum x0 -> x1, other arithmetic: none -> 7.97 us  [per_device(): feature_grad = jnp.sum(lax.all_gather(feature_grad, 'head'), axis=0)]
  transfers between devices with their start and end apart: 9 -> 9, of which waited for: 5 -> 4; matrix products, arithmetic and copies ran while one was open for 6% -> 7% of each run, Pallas kernels for 0% -> 0%
where the time goes in v1:
time: 542 us; the launch traced here: 541 us
  blocking collectives  251 us (46%)
  waiting for transfers between devices  165 us (30%)
  local copies, waits for them, and re-layouts  40.5 us (7%)
  other arithmetic  35.9 us (7%)
  matrix products  22.2 us (4%)
  between operations  16.1 us (3%)
  starting transfers between devices  10.5 us (2%)
    psum x1, blocking collectives, seq_total(): return lax.psum((stem_part, vector_part), 'seq')  251 us
    all_gather x1, waiting for transfers between devices, per_device(): feature_grad = jnp.sum(lax.all_gather(feature_grad, 'head'), axis=0)  112 us
    ppermute x4, waiting for transfers between devices, swapped(): return lax.ppermute(value, axis, pairs)  52.9 us
    unnamed x59, local copies, waits for them, and re-layouts  20.6 us
  transfers between devices with their start and end apart: 9, of which 4 were waited for; matrix products, arithmetic and copies ran while one was open for 7% of the time, Pallas kernels for 0%

profile of v1, /device:TPU:8, one launch (start us, length us, event | category | flops | bytes accessed | tf_op | source)
XLA Modules:
  0.0 541.3 jit_solution(2409160519575261496)
XLA Ops:
  8.1 4.0 collective-permute-start
  14.0 10.3 %copy.44 = bf16[3072,3,3,128]{0,3,2,1:T(8,128)(2,1)} copy(bf16[3072,3,3,128]{3,0,2,1:T(8,128)(2,1)} %param.15) | data formatting | bytes 14155776 | tf_op args[5]
  31.3 2.3 fusion
  36.8 2.9 collective-permute-start.3
  40.1 17.6 %collective-permute-done.3 = bf16[2,256,2,3,128]{4,1,3,2,0:T(8,128)(2,1)} collective-permute-done((bf16[2,256,2,3,128]{4,1,3,2,0:T(8,128)(2,1)S(1)}, bf16[2,256,2,3,128]{4,1,3,2,0:T(8,128)(2,1)}, u32[]{:S(2)}, u32[]{:S(2)}) %collective-permute-start.3) | collective-permute-done | bytes 786464 | tf_op jit(solution)/shard_map/ppermute | solution.py:17
  59.6 2.6 gather_fusion
  62.2 2.3 copy.48
  67.4 3.4 convolution_bitcast_fusion.1
  70.8 2.1 fusion.4
  72.9 1.9 copy.54
  76.6 2.4 copy.53
  79.0 3.3 pad_maximum_fusion
  82.3 3.1 copy.55
  85.7 9.3 %scatter_fusion = f32[8,128,2,3,128]{4,1,3,2,0:T(8,128)S(1)} fusion(f32[8,128,2,3,128]{4,1,3,2,0:T(8,128)S(1)} %broadcast_in_dim.47, s32[16]{0:T(128)S(1)} %fusion.24, f32[16,128,2,3,128]{4,1,3,2,0:T(8,128)} %copy.55), kind=kCustom, calls=%fused_computation.1 | custom fusion | flops 1572864 | bytes 18874432 | tf_op jit(solution)/shard_map/scatter-add | solution.py:184
  97.7 34.2 %collective-permute-done.4 = f32[2,256,2,3,128]{4,1,3,2,0:T(8,128)S(1)} collective-permute-done((f32[2,256,2,3,128]{4,1,3,2,0:T(8,128)S(1)}, f32[2,256,2,3,128]{4,1,3,2,0:T(8,128)S(1)}, u32[]{:S(2)}, u32[]{:S(2)}) %collective-permute-start.4) | collective-permute-done | bytes 1572896 | tf_op jit(solution)/shard_map/ppermute | solution.py:17
  136.3 3.9 convolution_bitcast_fusion
  140.5 2.1 maximum_convert_fusion
  142.5 2.1 copy.59
  144.7 8.4 %fusion.14 = f32[3072,1152]{1,0:T(8,128)} fusion(bf16[256,1152]{0,1:T(8,128)(2,1)} %bitcast.150, f32[256,3072]{1,0:T(8,128)S(1)} %copy-done.5, f32[3072]{0:T(1024)S(1)} %copy-done.17, f32[3072]{0:T(1024)S(1)} %broadcast_add_fusion), kind=kOutput, calls=%fused_computation.48 | convolution fusion | flops 1814298624 | bytes 17915904 | tf_op jit(solution)/shard_map/dot_general | solution.py:196
  153.2 112.0 %all-gather.3.cloned.1.call-done = f32[1024,3072]{1,0:T(8,128)} async-done(((f32[256,3072]{1,0:T(8,128)}), f32[1024,3072]{1,0:T(8,128)}) %all-gather.3.cloned.1.call-update) | async-done | bytes 12582928 | tf_op jit(solution)/shard_map/all_gather | solution.py:208
  265.2 8.0 %reduce_sum.142 = f32[256,3072]{1,0:T(8,128)} reduce(f32[4,256,3072]{2,1,0:T(8,128)} %bitcast.136, f32[]{:T(128)} %constant.98.clone.1), dimensions={0}, to_apply=%region_10.11 | reduce | flops 2359296 | bytes 15728644 | tf_op jit(solution)/shard_map/reduce_sum | solution.py:208
  273.1 2.8 fusion.26
  279.1 251.1 %psum.15 = f32[3,768]{1,0:T(4,128)} all-reduce(f32[3,768]{1,0:T(4,128)S(1)} %pad_maximum_fusion.4), channel_id=1, replica_groups=mesh['seq'=64,'head'=4] {'seq'}, use_global_device_ids=true, to_apply=%region_17.18 | all-reduce | flops 2304 | bytes 18432 | tf_op jit(solution)/shard_map/psum | solution.py:112
  532.0 1.9 copy.72
  (134 shorter events, 31.6 us)
Async XLA Ops:
  8.0 19.1 %copy-start = (bf16[192,3072]{1,0:T(8,128)(2,1)S(1)}, bf16[192,3072]{1,0:T(8,128)(2,1)}, u32[]{:S(2)}) copy-start(bf16[192,3072]{1,0:T(8,128)(2,1)} %param.11) | copy-start | bytes 3538948
  8.0 257.1 %all-gather.3.cloned.1.call-start = ((), (), s32[]{:S(2)}) async-start(), calls=%async_computation.3 | async-start | bytes 15728640 | tf_op jit(solution)/shard_map/all_gather | solution.py:208
  8.1 16.3 %collective-permute-start = (bf16[1,16,1024]{2,1,0:T(8,128)(2,1)}, bf16[1,16,1024]{2,1,0:T(8,128)(2,1)S(1)}, u32[]{:S(2)}, u32[]{:S(2)}) collective-permute-start(bf16[1,16,1024]{2,1,0:T(8,128)(2,1)} %param.10), channel_id=1, source_target_pairs={{0,8},{4,12},{8,16},{12,20},{16,24},{20,28},{24,32},{28,36},{32,40... | collective-permute-start | bytes 98312 | tf_op jit(solution)/shard_map/ppermute | solution.py:23
  12.0 12.3 %collective-permute-start.1 = (bf16[1,16,1024]{2,1,0:T(8,128)(2,1)}, bf16[1,16,1024]{2,1,0:T(8,128)(2,1)S(1)}, u32[]{:S(2)}, u32[]{:S(2)}) collective-permute-start(bf16[1,16,1024]{2,1,0:T(8,128)(2,1)} %param.10), channel_id=1, source_target_pairs={{8,0},{12,4},{16,8},{20,12},{24,16},{28,20},{32,24},{36,28},{40,32... | collective-permute-start | bytes 98312 | tf_op jit(solution)/shard_map/ppermute | solution.py:23
  14.0 10.3 %copy-start.18 = (bf16[1,16,1024]{2,1,0:T(8,128)(2,1)S(1)}, bf16[1,16,1024]{2,1,0:T(8,128)(2,1)}, u32[]{:S(2)}) copy-start(bf16[1,16,1024]{2,1,0:T(8,128)(2,1)} %param.10) | copy-start | bytes 98308
  24.3 2.8 copy-start.19
  27.1 3.3 slice-start.2
  27.8 3.5 slice-start.3
  31.3 3.3 copy-start.20
  33.9 5.9 %copy-start.21 = (f32[128]{0:T(128)S(1)}, f32[128]{0:T(128)}, u32[]{:S(2)}) copy-start(f32[128]{0:T(128)} %param.16) | copy-start | bytes 1540
  34.8 1.8 collective-permute-start.2
  35.5 29.5 %copy-start.15 = (bf16[2,2,1,8,8,3,128]{6,4,3,5,1,0,2:T(8,128)(2,1)}, bf16[2,2,1,8,8,3,128]{6,4,3,5,1,0,2:T(8,128)(2,1)S(1)}, u32[]{:S(2)}) copy-start(bf16[2,2,1,8,8,3,128]{6,4,3,5,1,0,2:T(8,128)(2,1)S(1)} %copy.51) | copy-start | bytes 589828
  36.8 20.9 %collective-permute-start.3 = (bf16[2,256,2,3,128]{4,1,3,2,0:T(8,128)(2,1)S(1)}, bf16[2,256,2,3,128]{4,1,3,2,0:T(8,128)(2,1)}, u32[]{:S(2)}, u32[]{:S(2)}) collective-permute-start(bf16[2,256,2,3,128]{4,1,3,2,0:T(8,128)(2,1)S(1)} %pad_maximum_fusion.2), channel_id=1, source_target_pairs={{0,8},{4,12},{8,0},{12,4},{16,24},{20,28},{24,16},{28,20},{32,40},... | collective-permute-start | bytes 2359304 | tf_op jit(solution)/shard_map/ppermute | solution.py:17
  95.7 36.6 %copy-start.12 = (bf16[4,3,64,512]{3,2,1,0:T(8,128)(2,1)S(1)}, bf16[4,3,64,512]{3,2,1,0:T(8,128)(2,1)}, u32[]{:S(2)}) copy-start(bf16[4,3,64,512]{3,2,1,0:T(8,128)(2,1)} %copy-done.11) | copy-start | bytes 2359300
  95.9 36.0 %collective-permute-start.4 = (f32[2,256,2,3,128]{4,1,3,2,0:T(8,128)S(1)}, f32[2,256,2,3,128]{4,1,3,2,0:T(8,128)S(1)}, u32[]{:S(2)}, u32[]{:S(2)}) collective-permute-start(f32[2,256,2,3,128]{4,1,3,2,0:T(8,128)S(1)} %copy.57), channel_id=1, source_target_pairs={{0,8},{4,12},{8,0},{12,4},{16,24},{20,28},{24,16},{28,20},{32,40},... | collective-permute-start | bytes 4718600 | tf_op jit(solution)/shard_map/ppermute | solution.py:17
  131.9 4.5 slice-start
  132.2 2.6 copy-start.9
  132.2 4.1 slice-start.1
  132.2 2.4 collective-permute-start.5
  140.2 4.5 copy-start.5
  140.2 390.0 %reduce-scatter.2.cloned.1.call-start = ((), (), s32[]{:S(2)}) async-start(), calls=%async_computation.1 | async-start | bytes 14376960 | tf_op jit(solution)/shard_map/reduce_scatter | solution.py:195
  153.1 378.9 %all-reduce.2.cloned.1.call-start = ((), (), s32[]{:S(2)}) async-start(), calls=%async_computation.2 | async-start | bytes 1179648 | tf_op jit(solution)/shard_map/psum | solution.py:112
  265.2 8.0 %copy-start.3 = (f32[256,3072]{1,0:T(8,128)S(1)}, f32[256,3072]{1,0:T(8,128)}, u32[]{:S(2)}) copy-start(f32[256,3072]{1,0:T(8,128)} %copy-done.2) | copy-start | bytes 9437188
  275.9 257.9 %copy-start.1 = (bf16[192,3072]{1,0:T(8,128)(2,1)S(1)}, bf16[192,3072]{1,0:T(8,128)(2,1)}, u32[]{:S(2)}) copy-start(bf16[192,3072]{1,0:T(8,128)(2,1)} %param.11) | copy-start | bytes 3538948
  (12 other events, 18.3 us)
Sparse Core Ops, SparseCore 0:
  140.3 124.7 all-gather.2
Sparse Core Ops, SparseCore 1:
  153.2 168.2 reduce-scatter.1
  325.4 180.1 all-reduce.1
